TPU v7x, 512 devices: a whole 4x8x8 slice. The times are simulated.
512 devices in a mesh: sub: 4 (over z_lo), row: 16 (over z_hi, x, core), col: 8 (over y).
Axes of the slice: x: 4, y: 8, z: 8 (z_hi: 2, z_lo: 4; z = z_hi * 4 + z_lo), core: 2. Of those that a mesh axis runs over, the one named last changes fastest.
Arguments:
- child_update: bfloat16 [32768, 8192], P(('sub', 'row'), 'col'), may hold values from -2.8 to 2.8, as said below
- parent_front: bfloat16 [16384, 16384], P('row', ('sub', 'col')), may hold values from -2.8 to 256, as said below
- tile_map: int32 [4, 64], replicated, may hold values from -1 to 127, as said below
Outputs:
- front_out: float32 [16384, 16384], P('row', ('sub', 'col'))
Inputs may be any that keep to these rules, and one draw needn't show every extreme that they name: Live tiles of a child come first, a whole multiple of 16 of them, at least max(1, 2) * 16; then -1. At least one child has all 64 tiles live. Within one child the parent tiles are distinct, and (tile_map[s, j] // 4) % 16 == j % 16 for every live j. `child_update`: each child's update, in logical order, is a symmetric matrix. `parent_front`: symmetric in logical order, with diagonal entries between 64 and 256; the assembled leading 4 x 4 tiles are positive definite.
All inputs are finite; a program needn't handle non-finite values.
Results may differ from a plain program's by a relative error of at most 0.0008.
Values may be sent and summed in bfloat16 or wider, within the bound.
A program may use at most 64 MiB of HBM per device.

v0:
```python
import jax
import jax.numpy as jnp
from jax import lax
from jax.sharding import PartitionSpec as P

TILE = 128
PANEL = 4
precise = lax.Precision.HIGHEST


def from_root(x, axis, root):
    mine = lax.axis_index(axis) == root
    return lax.psum(jnp.where(mine, x, jnp.zeros_like(x)), axis)


def body(child_update, parent_front, tile_map):
    tile_len = TILE
    panel_tiles = PANEL
    panel_width = panel_tiles * tile_len
    sub_count = lax.axis_size("sub")
    row_count = lax.axis_size("row")
    col_count = lax.axis_size("col")
    sub_id = lax.axis_index("sub")
    row_id = lax.axis_index("row")
    col_id = lax.axis_index("col")
    block_id = sub_id * col_count + col_id
    child_rows = child_update.shape[0] // tile_len
    child_cols = child_update.shape[1] // tile_len
    front_rows = parent_front.shape[0] // tile_len
    own_map = lax.dynamic_index_in_dim(tile_map, sub_id, 0, keepdims=False)
    own_cols = lax.dynamic_index_in_dim(
        own_map.reshape(child_cols, col_count), col_id, 1, keepdims=False
    )
    live_cols = own_cols >= 0
    destination = jnp.floor_divide(jnp.floor_divide(own_cols, panel_tiles), col_count)
    slot_index = jnp.remainder(own_cols, panel_tiles)
    dest_hit = destination[None, :] == jnp.arange(sub_count, dtype=jnp.int32)[:, None]
    slot_hit = slot_index[None, :] == jnp.arange(panel_tiles, dtype=jnp.int32)[:, None]
    select = (live_cols[None, None, :] & dest_hit[:, None, :] & slot_hit[None, :, :]).astype(
        jnp.bfloat16
    )
    column_slabs = child_update.reshape(child_rows * tile_len, child_cols, tile_len)
    payload = jnp.einsum(
        "dqk,rky->dqry", select, column_slabs, preferred_element_type=jnp.float32
    ).astype(jnp.bfloat16)
    maps_rows = lax.dynamic_index_in_dim(
        tile_map.reshape(sub_count, child_rows, row_count), row_id, 2, keepdims=False
    )
    local_row = jnp.floor_divide(
        jnp.floor_divide(maps_rows, panel_tiles), row_count
    ) * panel_tiles + jnp.remainder(maps_rows, panel_tiles)
    row_hit = (maps_rows[:, :, None] >= 0) & (
        local_row[:, :, None] == jnp.arange(front_rows, dtype=jnp.int32)[None, None, :]
    )
    place_row = row_hit.astype(jnp.bfloat16)
    arrived = lax.all_to_all(payload, "sub", split_axis=0, concat_axis=0, tiled=True)
    slot_count = arrived.shape[1]
    grid = arrived.reshape(sub_count, slot_count, child_rows, tile_len, tile_len)
    spread = jnp.einsum("ska,sqkyx->ayqx", place_row, grid, preferred_element_type=jnp.float32)
    placed = spread.reshape(front_rows * tile_len, slot_count * tile_len)
    front_local = parent_front.astype(jnp.float32) + placed
    top_block = from_root(front_local[:panel_width].astype(jnp.bfloat16), "row", 0).astype(
        jnp.float32
    )
    panel_rows, leading = (
        from_root(front_local.astype(jnp.bfloat16), ("sub", "col"), 0).astype(front_local.dtype),
        from_root(top_block.astype(jnp.bfloat16), ("sub", "col"), 0).astype(top_block.dtype),
    )
    lower_factor = jnp.tril(jnp.linalg.cholesky(leading))
    identity = jnp.eye(panel_width, dtype=jnp.float32)
    inverse = jax.scipy.linalg.solve_triangular(lower_factor, identity, lower=True)
    factor_rows = jnp.dot(
        panel_rows, inverse.T, precision=precise, preferred_element_type=jnp.float32
    )
    head_rows = jnp.where(row_id == 0, lower_factor, factor_rows[:panel_width])
    factor_rows = jnp.concatenate([head_rows, factor_rows[panel_width:]], axis=0)
    source_row = jnp.remainder(block_id, row_count)
    first_row = jnp.floor_divide(block_id, row_count) * panel_width
    factor_piece = lax.dynamic_slice_in_dim(factor_rows, first_row, panel_width, 0)
    column_side = from_root(factor_piece.astype(jnp.bfloat16), "row", source_row).astype(
        factor_piece.dtype
    )
    update = jnp.dot(
        factor_rows, column_side.T, precision=precise, preferred_element_type=jnp.float32
    )
    keep_rows = (jnp.arange(front_rows * tile_len) >= panel_width) | (row_id != 0)
    trailing = front_local - jnp.where(keep_rows[:, None], update, 0.0)
    return jnp.where(block_id == 0, factor_rows, trailing)


def solution(mesh):
    in_specs = (P(("sub", "row"), "col"), P("row", ("sub", "col")), P())
    out_specs = P("row", ("sub", "col"))
    return jax.shard_map(body, mesh=mesh, in_specs=in_specs, out_specs=out_specs, check_vma=False)
```

profile of v0, /device:TPU:1, one launch (start us, length us, event | category | flops | bytes accessed | tf_op | source)
XLA Modules:
  0.0 940.0 jit_solution(14643982582038537792)
XLA Ops:
  6.5 0.7 fusion.65
  7.5 1.5 copy.51
  9.1 2.0 convolution_convert_fusion
  11.1 7.9 all-to-all-start
  19.5 1.5 copy.23
  21.0 45.7 %all-to-all-done = bf16[4,4,512,128]{3,1,2,0:T(4,128)(2,1)S(1)} async-done(((bf16[4,4,512,128]{3,1,2,0:T(4,128)(2,1)}), bf16[4,4,512,128]{3,1,2,0:T(4,128)(2,1)S(1)}, u32[]{:S(2)}, u32[]{:S(2)}) %all-to-all-start) | async-done | bytes 2097184 | tf_op jit(solution)/shard_map/all_to_all | solution.py:56
  66.8 5.0 fusion.3
  71.8 2.0 copy.28
  73.8 1.7 broadcast_select_fusion
  75.6 0.8 slice_select_fusion.1
  76.5 187.6 %all-reduce.6.cloned.1.call-done = bf16[512,512]{0,1:T(8,128)(2,1)} async-done(((bf16[512,512]{0,1:T(8,128)(2,1)}), bf16[512,512]{0,1:T(8,128)(2,1)}) %all-reduce.6.cloned.1.call-update) | async-done | bytes 524304 | tf_op jit(solution)/shard_map/psum | solution.py:13
  264.0 1.9 broadcast_select_fusion.1
  265.9 0.5 all-reduce.8.cloned.1.call-start
  266.5 0.8 iota_compare_fusion
  267.3 1.2 fusion.28
  268.4 290.1 %all-reduce.10.cloned.1.call-done = (bf16[512,512]{0,1:T(8,128)(2,1)}, bf16[1024,512]{0,1:T(8,128)(2,1)}) async-done(((bf16[512,512]{0,1:T(8,128)(2,1)}, bf16[1024,512]{0,1:T(8,128)(2,1)}), (bf16[512,512]{0,1:T(8,128)(2,1)}, bf16[1024,512]{0,1:T(8,128)(2,1)})) %all-reduce.10.cloned.1.call-update) | async-done | bytes 1572880 | tf_op jit(solution)/shard_map/psum | solution.py:13
  558.5 1.3 copy.29
  559.7 1.2 fusion.17
  560.9 1.0 copy-done.4
  561.9 11.7 %cholesky.104 = f32[128,128]{1,0:T(8,128)S(1)} custom-call(f32[128,128]{1,0:T(8,128)S(1)} %cholesky.266), custom_call_target="Cholesky" | custom-call | tf_op jit(solution)/shard_map/jit(cholesky)/cholesky | solution.py:69
  573.6 0.7 copy.30
  574.4 9.8 %custom-call.31 = f32[1,128,128]{1,2,0:T(8,128)S(1)} custom-call(f32[1,128,128]{2,1,0:T(8,128)S(1)} %get-tuple-element.42), custom_call_target="InvertDiagBlocksLowerTriangular" | custom-call | tf_op jit(solution)/shard_map/jit(cholesky)/cholesky | solution.py:69
  584.2 1.2 fusion.34
  585.6 1.3 convolution_subtract_fusion.3
  586.9 11.7 %cholesky.217 = f32[128,128]{1,0:T(8,128)S(1)} custom-call(f32[128,128]{1,0:T(8,128)S(1)} %cholesky.270), custom_call_target="Cholesky" | custom-call | tf_op jit(solution)/shard_map/jit(cholesky)/cholesky | solution.py:69
  598.6 0.7 copy.32
  599.3 10.6 %custom-call.32 = f32[1,128,128]{1,2,0:T(8,128)} custom-call(f32[1,128,128]{2,1,0:T(8,128)S(1)} %get-tuple-element.40), custom_call_target="InvertDiagBlocksLowerTriangular" | custom-call | tf_op jit(solution)/shard_map/jit(cholesky)/cholesky | solution.py:69
  609.9 1.0 cholesky.224
  610.9 0.8 constant_dynamic-update-slice_fusion.3
  611.7 1.2 convolution_dynamic-update-slice_fusion
  612.9 1.5 convolution_subtract_fusion.4
  614.4 11.7 %cholesky.238 = f32[128,128]{1,0:T(8,128)S(1)} custom-call(f32[128,128]{1,0:T(8,128)S(1)} %cholesky.275), custom_call_target="Cholesky" | custom-call | tf_op jit(solution)/shard_map/jit(cholesky)/cholesky | solution.py:69
  626.3 9.8 %custom-call.33 = f32[1,128,128]{1,2,0:T(8,128)S(1)} custom-call(f32[1,128,128]{2,1,0:T(8,128)S(1)} %get-tuple-element.38), custom_call_target="InvertDiagBlocksLowerTriangular" | custom-call | tf_op jit(solution)/shard_map/jit(cholesky)/cholesky | solution.py:69
  636.4 1.3 convolution_subtract_fusion.5
  637.7 11.9 %cholesky.255 = f32[128,128]{1,0:T(8,128)S(1)} custom-call(f32[128,128]{1,0:T(8,128)S(1)} %convolution_subtract_fusion.5), custom_call_target="Cholesky" | custom-call | tf_op jit(solution)/shard_map/jit(cholesky)/cholesky | solution.py:69
  649.8 0.7 compare_reduce_fusion.3
  650.5 0.7 compare_reduce_fusion.2
  651.2 0.7 compare_reduce_fusion.1
  651.9 0.6 compare_reduce_fusion
  655.1 1.1 fusion.18
  656.2 14.7 %while.1 = (s32[]{:T(128)}, f32[512,512]{0,1:T(8,128)}, s32[4,2]{0,1:T(2,128)S(1)}, f32[4,128,128]{2,1,0:T(8,128)}, s32[]{:T(128)}) while((s32[]{:T(128)}, f32[512,512]{0,1:T(8,128)}, s32[4,2]{0,1:T(2,128)S(1)}, f32[4,128,128]{2,1,0:T(8,128)}, s32[]{:T(128)}) %tuple.28), condition=%wide.while_cond, body=%wide.while_body.sunk | while | flops 2 | bytes 393329 | solution.py:71
  656.3 0.6 fusion.81
  656.8 2.3 dynamic-slice.7
  659.2 0.6 bitcast_dynamic-update-slice_fusion.2
  659.9 0.6 fusion.81
  660.5 2.3 dynamic-slice.7
  662.9 0.6 bitcast_dynamic-update-slice_fusion.2
  663.6 0.6 fusion.81
  664.2 2.3 dynamic-slice.7
  666.6 0.6 bitcast_dynamic-update-slice_fusion.2
  667.3 0.6 fusion.81
  667.9 2.2 dynamic-slice.7
  670.2 0.6 bitcast_dynamic-update-slice_fusion.2
  670.9 40.1 %custom-call.34 = f32[4,128,128]{1,2,0:T(8,128)S(1)} custom-call(f32[4,128,128]{2,1,0:T(8,128)} %get-tuple-element.12), custom_call_target="InvertDiagBlocksLowerTriangular" | custom-call | tf_op jit(solution)/shard_map/jit(_solve_triangular)/triangular_solve | solution.py:71
  711.0 1.1 fusion.30
  712.1 1.4 convolution_subtract_fusion.1
  714.0 1.5 convolution_subtract_fusion
  715.9 1.7 convolution_subtract_fusion.2
  718.1 1.8 fusion.9
  720.2 1.0 copy-done
  721.2 1.1 fusion.24
  722.3 202.5 %all-reduce.8.cloned.1.call-done = bf16[512,512]{0,1:T(8,128)(2,1)} async-done(((bf16[512,512]{0,1:T(8,128)(2,1)}), bf16[512,512]{0,1:T(8,128)(2,1)}) %all-reduce.8.cloned.1.call-update) | async-done | bytes 524304 | tf_op jit(solution)/shard_map/psum | solution.py:13
  924.8 5.6 subtract_select_fusion
  930.4 2.9 copy.41
  (59 shorter events, 3.9 us)
Async XLA Ops:
  11.1 7.9 copy-start.6
  11.1 55.7 %all-to-all-start = ((bf16[4,4,512,128]{3,1,2,0:T(4,128)(2,1)}), bf16[4,4,512,128]{3,1,2,0:T(4,128)(2,1)S(1)}, u32[]{:S(2)}, u32[]{:S(2)}) async-start(bf16[4,4,512,128]{3,1,2,0:T(4,128)(2,1)} %convolution_convert_fusion), calls=%async_computation | async-start | bytes 4194304 | tf_op jit(solution)/shard_map/all_to_all | solution.py:56
  19.0 245.0 %all-reduce.6.cloned.1.call-start = ((), (), s32[]{:S(2)}) async-start(), calls=%async_computation.1 | async-start | bytes 1048576 | tf_op jit(solution)/shard_map/psum | solution.py:13
  21.0 52.8 %copy-start.3 = (bf16[1024,512]{0,1:T(8,128)(2,1)}, bf16[1024,512]{0,1:T(8,128)(2,1)S(1)}, u32[]{:S(2)}) copy-start(bf16[1024,512]{0,1:T(8,128)(2,1)S(1)} %copy.23) | copy-start | bytes 3145732
  76.4 482.0 %all-reduce.10.cloned.1.call-start = ((), (), s32[]{:S(2)}) async-start(), calls=%async_computation.3 | async-start | bytes 3145728 | tf_op jit(solution)/shard_map/psum | solution.py:13
  265.9 658.8 %all-reduce.8.cloned.1.call-start = ((), (), s32[]{:S(2)}) async-start(), calls=%async_computation.2 | async-start | bytes 1048576 | tf_op jit(solution)/shard_map/psum | solution.py:13
  560.9 1.0 copy-start.4
  649.8 6.4 copy-start.1
  713.5 4.5 copy-start.5
  718.1 1.8 copy-start.2
  720.2 1.0 copy-start
Sparse Core Ops, SparseCore 0:
  76.5 187.4 all-reduce.5
  267.0 291.4 all-reduce.9
  722.4 202.3 all-reduce.7
where the time goes:
time: 946 us; the launch traced here: 940 us
  waiting for transfers between devices  726 us (77%)
  other arithmetic  130 us (14%)
  local copies, waits for them, and re-layouts  30.8 us (3%)
  matrix products  28.2 us (3%)
  between operations  16.3 us (2%)
    psum x3, waiting for transfers between devices, from_root(): return lax.psum(jnp.where(mine, x, jnp.zeros_like(x)), axis)  680 us
    another operation x15, other arithmetic, body(): lower_factor = jnp.tril(jnp.linalg.cholesky(leading))  80.1 us
    all_to_all x1, waiting for transfers between devices, body(): lax.all_to_all(payload, 'sub', split_axis=0, concat_axis=0, tiled=True)  45.7 us
    another operation x3, other arithmetic, body(): jax.scipy.linalg.solve_triangular(lower_factor, identity, lower=True)  41.2 us
  transfers between devices with their start and end apart: 4, of which 4 were waited for; matrix products, arithmetic and copies ran while one was open for 0% of the time, Pallas kernels for 0%

commit v1 on v0

--- a/solution.py
+++ b/solution.py
@@ -8,9 +8,14 @@
 precise = lax.Precision.HIGHEST
 
 
+def forms_remake(incoming_x, shard_axis):
+    y = jnp.sum(lax.all_gather(incoming_x, shard_axis), axis=0)
+    return y
+
+
 def from_root(x, axis, root):
     mine = lax.axis_index(axis) == root
-    return lax.psum(jnp.where(mine, x, jnp.zeros_like(x)), axis)
+    return forms_remake(jnp.where(mine, x, jnp.zeros_like(x)), shard_axis=axis)
 
 
 def body(child_update, parent_front, tile_map):

time: 946 us -> 909 us (0.961)
  waiting for transfers between devices: 726 us -> 668 us
  other arithmetic: 130 us -> 160 us
  local copies, waits for them, and re-layouts: 30.8 us -> 21.3 us
    psum x3 -> x0, waiting for transfers between devices: 680 us -> none  [from_root(): return lax.psum(jnp.where(mine, x, jnp.zeros_like(x)), axis)]
    all_gather x0 -> x4, waiting for transfers between devices: none -> 620 us  [forms_remake(): y = jnp.sum(lax.all_gather(incoming_x, shard_axis), axis=0)]
    reduce_sum x0 -> x4, other arithmetic: none -> 31 us  [forms_remake(): y = jnp.sum(lax.all_gather(incoming_x, shard_axis), axis=0)]
  transfers between devices with their start and end apart: 4 -> 5, of which waited for: 4 -> 5; matrix products, arithmetic and copies ran while one was open for 0% -> 18% of each run, Pallas kernels for 0% -> 0%
where the time goes in v1:
time: 909 us; the launch traced here: 902 us
  waiting for transfers between devices  668 us (73%)
  other arithmetic  160 us (18%)
  matrix products  28.4 us (3%)
  local copies, waits for them, and re-layouts  21.3 us (2%)
  between operations  16 us (2%)
    all_gather x4, waiting for transfers between devices, forms_remake(): y = jnp.sum(lax.all_gather(incoming_x, shard_axis), axis=0)  620 us
    another operation x15, other arithmetic, body(): lower_factor = jnp.tril(jnp.linalg.cholesky(leading))  79.4 us
    all_to_all x1, waiting for transfers between devices, body(): lax.all_to_all(payload, 'sub', split_axis=0, concat_axis=0, tiled=True)  47.2 us
    another operation x3, other arithmetic, body(): jax.scipy.linalg.solve_triangular(lower_factor, identity, lower=True)  41.9 us
    reduce_sum x4, other arithmetic, forms_remake(): y = jnp.sum(lax.all_gather(incoming_x, shard_axis), axis=0)  31 us
  transfers between devices with their start and end apart: 5, of which 5 were waited for; matrix products, arithmetic and copies ran while one was open for 18% of the time, Pallas kernels for 0%

profile of v1, /device:TPU:1, one launch (start us, length us, event | category | flops | bytes accessed | tf_op | source)
XLA Modules:
  0.0 901.6 jit_solution(17305398417554603714)
XLA Ops:
  6.5 0.7 fusion.65
  7.5 1.5 copy.27
  9.1 2.0 convolution_convert_fusion
  11.1 7.9 all-to-all-start
  19.5 47.2 %all-to-all-done = bf16[4,4,512,128]{3,1,2,0:T(4,128)(2,1)S(1)} async-done(((bf16[4,4,512,128]{3,1,2,0:T(4,128)(2,1)}), bf16[4,4,512,128]{3,1,2,0:T(4,128)(2,1)S(1)}, u32[]{:S(2)}, u32[]{:S(2)}) %all-to-all-start) | async-done | bytes 2097184 | tf_op jit(solution)/shard_map/all_to_all | solution.py:61
  66.8 3.7 fusion.3
  70.5 1.4 copy.20
  71.8 1.4 broadcast_select_fusion
  73.3 0.9 slice_select_fusion.1
  74.2 117.2 %all-gather.9.cloned.1.call-done = bf16[8192,512]{1,0:T(8,128)(2,1)} async-done(((bf16[512,512]{1,0:T(8,128)(2,1)}), bf16[8192,512]{1,0:T(8,128)(2,1)}) %all-gather.9.cloned.1.call-update) | async-done | bytes 8388624 | tf_op jit(solution)/shard_map/all_gather | solution.py:12
  191.4 4.8 reduce_sum.48
  196.2 0.8 broadcast_select_fusion.1
  197.1 0.7 all-gather.13.cloned.1.call-update
  197.9 0.8 iota_compare_fusion
  198.7 1.1 fusion.28
  199.8 188.2 %all-gather.11.cloned.1.call-done = bf16[16384,512]{1,0:T(8,128)(2,1)} async-done(((bf16[512,512]{1,0:T(8,128)(2,1)}), bf16[16384,512]{1,0:T(8,128)(2,1)}) %all-gather.11.cloned.1.call-update) | async-done | bytes 16777232 | tf_op jit(solution)/shard_map/all_gather | solution.py:12
  388.0 9.3 %reduce_sum.49 = bf16[512,512]{1,0:T(8,128)(2,1)S(1)} reduce(bf16[32,512,512]{2,1,0:T(8,128)(2,1)} %bitcast.91, bf16[]{:T(256)} %constant.264.clone.1), dimensions={0}, to_apply=%region_1.2 | reduce | flops 8126464 | bytes 17301506 | tf_op jit(solution)/shard_map/reduce_sum | solution.py:12
  397.5 1.2 copy.22
  398.7 1.4 fusion.17
  400.1 1.0 copy-done.5
  401.1 11.7 %cholesky.104 = f32[128,128]{1,0:T(8,128)S(1)} custom-call(f32[128,128]{1,0:T(8,128)S(1)} %cholesky.266), custom_call_target="Cholesky" | custom-call | tf_op jit(solution)/shard_map/jit(cholesky)/cholesky | solution.py:74
  412.9 9.8 %custom-call.31 = f32[1,128,128]{1,2,0:T(8,128)S(1)} custom-call(f32[1,128,128]{2,1,0:T(8,128)S(1)} %get-tuple-element.36), custom_call_target="InvertDiagBlocksLowerTriangular" | custom-call | tf_op jit(solution)/shard_map/jit(cholesky)/cholesky | solution.py:74
  422.7 1.2 constant_dynamic-update-slice_fusion
  424.0 1.3 convolution_subtract_fusion.3
  425.3 11.7 %cholesky.217 = f32[128,128]{1,0:T(8,128)S(1)} custom-call(f32[128,128]{1,0:T(8,128)S(1)} %cholesky.270), custom_call_target="Cholesky" | custom-call | tf_op jit(solution)/shard_map/jit(cholesky)/cholesky | solution.py:74
  437.0 10.0 %custom-call.32 = f32[1,128,128]{1,2,0:T(8,128)S(1)} custom-call(f32[1,128,128]{2,1,0:T(8,128)S(1)} %get-tuple-element.33), custom_call_target="InvertDiagBlocksLowerTriangular" | custom-call | tf_op jit(solution)/shard_map/jit(cholesky)/cholesky | solution.py:74
  447.0 0.3 convolution_dynamic-update-slice_fusion
  447.3 1.3 convolution_subtract_fusion.4
  448.6 11.7 %cholesky.238 = f32[128,128]{1,0:T(8,128)S(1)} custom-call(f32[128,128]{1,0:T(8,128)S(1)} %cholesky.275), custom_call_target="Cholesky" | custom-call | tf_op jit(solution)/shard_map/jit(cholesky)/cholesky | solution.py:74
  460.3 9.8 %custom-call.33 = f32[1,128,128]{1,2,0:T(8,128)S(1)} custom-call(f32[1,128,128]{2,1,0:T(8,128)S(1)} %get-tuple-element.30), custom_call_target="InvertDiagBlocksLowerTriangular" | custom-call | tf_op jit(solution)/shard_map/jit(cholesky)/cholesky | solution.py:74
  470.4 1.2 convolution_subtract_fusion.5
  471.6 11.7 %cholesky.255 = f32[128,128]{1,0:T(8,128)S(1)} custom-call(f32[128,128]{1,0:T(8,128)S(1)} %convolution_subtract_fusion.5), custom_call_target="Cholesky" | custom-call | tf_op jit(solution)/shard_map/jit(cholesky)/cholesky | solution.py:74
  483.3 0.6 compare_reduce_fusion.3
  483.9 0.6 compare_reduce_fusion.2
  485.7 0.6 compare_reduce_fusion.1
  486.9 0.2 select_reduce_fusion
  487.1 0.7 compare_reduce_fusion
  488.5 1.1 fusion.18
  489.6 13.4 %while.1 = (s32[]{:T(128)}, f32[512,512]{1,0:T(8,128)}, s32[4,2]{0,1:T(2,128)S(1)}, f32[4,128,128]{2,1,0:T(8,128)}, s32[]{:T(128)}) while((s32[]{:T(128)}, f32[512,512]{1,0:T(8,128)}, s32[4,2]{0,1:T(2,128)S(1)}, f32[4,128,128]{2,1,0:T(8,128)}, s32[]{:T(128)}) %tuple.30), condition=%wide.while_cond, body=%wide.while_body.sunk | while | flops 2 | bytes 132205 | solution.py:76
  489.7 0.5 fusion.81
  490.2 2.8 bitcast_dynamic-update-slice_fusion.2
  493.0 0.5 fusion.81
  493.6 2.8 bitcast_dynamic-update-slice_fusion.2
  496.4 0.5 fusion.81
  496.9 2.8 bitcast_dynamic-update-slice_fusion.2
  499.8 0.5 fusion.81
  500.3 2.7 bitcast_dynamic-update-slice_fusion.2
  503.0 40.7 %custom-call.34 = f32[4,128,128]{1,2,0:T(8,128)} custom-call(f32[4,128,128]{2,1,0:T(8,128)} %get-tuple-element.12), custom_call_target="InvertDiagBlocksLowerTriangular" | custom-call | tf_op jit(solution)/shard_map/jit(_solve_triangular)/triangular_solve | solution.py:76
  543.7 1.2 fusion.30
  544.9 1.4 convolution_subtract_fusion.1
  546.3 1.3 fusion.42
  547.6 1.5 convolution_subtract_fusion
  549.2 0.4 fusion.40
  549.6 1.8 convolution_subtract_fusion.2
  551.4 1.1 fusion.39
  552.5 203.7 %all-gather.13.cloned.1.call-done = bf16[32768,512]{1,0:T(8,128)(2,1)} async-done(((bf16[1024,512]{1,0:T(8,128)(2,1)}), bf16[32768,512]{1,0:T(8,128)(2,1)}) %all-gather.13.cloned.1.call-update) | async-done | bytes 33554448 | tf_op jit(solution)/shard_map/all_gather | solution.py:12
  756.2 11.4 %reduce_sum.50 = bf16[1024,512]{1,0:T(8,128)(2,1)S(1)} reduce(bf16[32,1024,512]{2,1,0:T(8,128)(2,1)} %bitcast.88, bf16[]{:T(256)} %constant.264.clone.1), dimensions={0}, to_apply=%region_10.11 | reduce | flops 16252928 | bytes 34603008 | tf_op jit(solution)/shard_map/reduce_sum | solution.py:12
  767.6 3.1 fusion.9
  770.7 0.3 slice_select_fusion
  771.0 1.1 copy-done
  772.1 1.3 fusion.24
  773.4 110.6 %all-gather.15.cloned.1.call-done = bf16[8192,512]{1,0:T(8,128)(2,1)} async-done(((bf16[512,512]{1,0:T(8,128)(2,1)}), bf16[8192,512]{1,0:T(8,128)(2,1)}) %all-gather.15.cloned.1.call-update) | async-done | bytes 8388624 | tf_op jit(solution)/shard_map/all_gather | solution.py:12
  883.9 5.5 reduce_sum.51
  889.4 5.4 subtract_select_fusion
  (52 shorter events, 2.0 us)
Async XLA Ops:
  11.1 7.9 copy-start.8
  11.1 55.7 %all-to-all-start = ((bf16[4,4,512,128]{3,1,2,0:T(4,128)(2,1)}), bf16[4,4,512,128]{3,1,2,0:T(4,128)(2,1)S(1)}, u32[]{:S(2)}, u32[]{:S(2)}) async-start(bf16[4,4,512,128]{3,1,2,0:T(4,128)(2,1)} %convolution_convert_fusion), calls=%async_computation | async-start | bytes 4194304 | tf_op jit(solution)/shard_map/all_to_all | solution.py:61
  19.0 172.4 %all-gather.9.cloned.1.call-start = ((), (), s32[]{:S(2)}) async-start(), calls=%async_computation.1 | async-start | bytes 8912896 | tf_op jit(solution)/shard_map/all_gather | solution.py:12
  70.5 1.4 copy-start.4
  74.2 313.8 %all-gather.11.cloned.1.call-start = ((), (), s32[]{:S(2)}) async-start(), calls=%async_computation.2 | async-start | bytes 17301504 | tf_op jit(solution)/shard_map/all_gather | solution.py:12
  197.1 559.1 %all-gather.13.cloned.1.call-start = ((), (), s32[]{:S(2)}) async-start(), calls=%async_computation.3 | async-start | bytes 34603008 | tf_op jit(solution)/shard_map/all_gather | solution.py:12
  197.8 686.1 %all-gather.15.cloned.1.call-start = ((), (), s32[]{:S(2)}) async-start(), calls=%async_computation.4 | async-start | bytes 8912896 | tf_op jit(solution)/shard_map/all_gather | solution.py:12
  400.1 1.0 copy-start.5
  487.1 59.2 %copy-start.1 = (f32[512,512]{1,0:T(8,128)}, f32[512,512]{1,0:T(8,128)S(1)}, u32[]{:S(2)}) copy-start(f32[512,512]{1,0:T(8,128)S(1)} %get-tuple-element.28) | copy-start | bytes 3145732
  543.7 5.4 copy-start.7
  547.6 2.0 copy-start.3
  549.6 1.8 copy-start.6
  767.6 3.1 copy-start.2
  771.0 1.1 copy-start
Sparse Core Ops, SparseCore 0:
  74.3 117.0 all-gather.8
  197.2 190.7 all-gather.10
  390.1 366.0 all-gather.12
  773.5 110.4 all-gather.14
